TPU v7x, 32 devices: a whole 2x2x4 slice. The times are simulated.
32 devices in a mesh: dp: 4 (over y, x), ctx: 8 (over z, core).
Axes of the slice: x: 2, y: 2, z: 4, core: 2. Of those that a mesh axis runs over, the one named last changes fastest.
Arguments:
- query_rows: bfloat16 [4, 1024, 1024], P('dp', 'ctx'), may hold values from -0.59765625 to 0.59765625
- key_rows: bfloat16 [4, 1024, 1024], P('dp', 'ctx'), may hold values from -0.59765625 to 0.59765625
- value_rows: bfloat16 [4, 1024, 2048], P('dp', 'ctx'), may hold values from -6 to 6
- log_decay: bfloat16 [4, 1024, 1024], P('dp', 'ctx'), may hold values from -1 to 0, as said below
- out_grad: bfloat16 [4, 1024, 2048], P('dp', 'ctx'), may hold values from -1.796875 to 1.796875
- doc_ids: int32 [4, 1024], P('dp', 'ctx'), may hold values from 0 to 3, as said below
- block_order: int32 [4, 8, 4], P(None, 'ctx'), may hold values from 0 to 3, each once within a row
Outputs:
- attn_out: bfloat16 [4, 1024, 2048], P('dp', 'ctx')
- query_grad: bfloat16 [4, 1024, 1024], P('dp', 'ctx')
- key_grad: bfloat16 [4, 1024, 1024], P('dp', 'ctx')
- value_grad: bfloat16 [4, 1024, 2048], P('dp', 'ctx')
- decay_grad: bfloat16 [4, 1024, 1024], P('dp', 'ctx')
Inputs may be any that keep to these rules, and one draw needn't show every extreme that they name: `log_decay`: nonpositive. `doc_ids`: never falls along a pack; every document number of a pack is used; each document has 1 to 512 positions, one of them exactly 512 and one 8 or fewer. `block_order`: each row of a device's list names each of its 4 blocks once.
All inputs are finite; a program needn't handle non-finite values.
Results may differ from a plain program's by a relative error of at most 0.0015.
Values may be sent and summed in bfloat16 or wider, within the bound.
A program may use at most 192 MiB of HBM per device.

v0:
```python
import jax
import jax.numpy as jnp
from jax import lax
from jax.sharding import PartitionSpec as P

DK = 64
DV = 128
BLK = 32


HIGH = lax.Precision.HIGHEST


def prefix(part, axis, combine, identity, reverse):
    count = lax.axis_size(axis)
    place = lax.axis_index(axis)
    ahead = count - 1 - place if reverse else place
    gathered = jax.tree.map(lambda a: lax.all_gather(a, axis), part)
    state = jax.tree.map(lambda a, e: jnp.zeros_like(a) + jnp.asarray(e, a.dtype), part, identity)

    def one(hop, state):
        source = count - 1 - hop if reverse else hop
        return combine(
            state, jax.tree.map(lambda a: lax.dynamic_index_in_dim(a, source, 0, False), gathered)
        )

    return lax.fori_loop(0, ahead, one, state)


def prepare(query_b, key_b, value_b, decay_b, doc_row):
    row_count = query_b.shape[0]
    head_count = query_b.shape[1] // DK
    query_f = query_b.astype(jnp.float32).reshape(row_count, head_count, DK)
    key_f = key_b.astype(jnp.float32).reshape(row_count, head_count, DK)
    value_f = value_b.astype(jnp.float32).reshape(row_count, head_count, DV)
    cumul = jnp.cumsum(decay_b.astype(jnp.float32).reshape(row_count, head_count, DK), axis=0)
    total_log = cumul[-1]
    growth = jnp.exp(cumul)
    shrink = jnp.exp(-cumul)
    to_end = jnp.exp(total_log[None] - cumul)
    later_pos = lax.broadcasted_iota(jnp.int32, (row_count, row_count), 0)
    earlier_pos = lax.broadcasted_iota(jnp.int32, (row_count, row_count), 1)
    same_doc = ((later_pos >= earlier_pos) & (doc_row[:, None] == doc_row[None, :])).astype(
        jnp.float32
    )
    first_id = doc_row[0]
    last_id = doc_row[-1]
    in_first = (doc_row == first_id).astype(jnp.float32)[:, None, None]
    in_last = (doc_row == last_id).astype(jnp.float32)[:, None, None]
    query_t = query_f * growth
    key_t = key_f * shrink
    scores = jnp.einsum("thi,shi->hts", query_t, key_t, precision=HIGH) * same_doc[None]
    return {
        "query_f": query_f,
        "key_f": key_f,
        "value_f": value_f,
        "growth": growth,
        "shrink": shrink,
        "to_end": to_end,
        "same_doc": same_doc,
        "first_id": first_id,
        "last_id": last_id,
        "in_first": in_first,
        "in_last": in_last,
        "query_t": query_t,
        "key_t": key_t,
        "scores": scores,
        "decay_all": jnp.exp(total_log),
    }


def state_end(parts):
    return jnp.einsum(
        "shi,shj->hij",
        parts["key_f"] * parts["to_end"] * parts["in_last"],
        parts["value_f"],
        precision=HIGH,
    )


def start_grad(parts, grad_f):
    factor = DK ** (-0.5)
    return factor * jnp.einsum(
        "thi,thj->hij", parts["query_t"] * parts["in_first"], grad_f, precision=HIGH
    )


def finish(parts, grad_f, state_in, use_state, carry_in, use_carry):
    factor = DK ** (-0.5)
    head_w = parts["in_first"] * use_state
    tail_w = parts["in_last"] * use_carry
    attn_rows = factor * (
        jnp.einsum("hts,shj->thj", parts["scores"], parts["value_f"], precision=HIGH)
        + jnp.einsum("thi,hij->thj", parts["query_t"], state_in, precision=HIGH) * head_w
    )
    grad_scores = (
        jnp.einsum("thj,shj->hts", grad_f, parts["value_f"], precision=HIGH)
        * parts["same_doc"][None]
    )
    grad_query = (
        factor
        * parts["growth"]
        * (
            jnp.einsum("hts,shi->thi", grad_scores, parts["key_t"], precision=HIGH)
            + jnp.einsum("thj,hij->thi", grad_f, state_in, precision=HIGH) * head_w
        )
    )
    grad_value = (
        factor * jnp.einsum("hts,thj->shj", parts["scores"], grad_f, precision=HIGH)
        + jnp.einsum("shi,hij->shj", parts["key_f"] * parts["to_end"], carry_in, precision=HIGH)
        * tail_w
    )
    grad_key = (
        factor
        * parts["shrink"]
        * jnp.einsum("hts,thi->shi", grad_scores, parts["query_t"], precision=HIGH)
        + parts["to_end"]
        * jnp.einsum("hij,shj->shi", carry_in, parts["value_f"], precision=HIGH)
        * tail_w
    )
    grad_log = parts["query_f"] * grad_query - parts["key_f"] * grad_key
    sum_start = jnp.sum(grad_log * parts["in_first"], axis=0)
    return (attn_rows, grad_query, grad_key, grad_value, grad_log, sum_start)


def decay_grad_of(parts, grad_log, sums_in, use_carry):
    inside = jnp.einsum("ts,thi->shi", parts["same_doc"], grad_log, precision=HIGH)
    return inside + sums_in[None] * parts["in_last"] * use_carry


def select_tree(flag, yes_tree, no_tree):
    return tuple((jnp.where(flag, left, right) for left, right in zip(yes_tree, no_tree)))


def join_forward(before, follow):
    b_dec, b_state, b_first, b_last = before
    f_dec, f_state, f_first, f_last = follow
    joined = ((f_first == f_last) & (b_last == f_first)).astype(jnp.float32)
    merged = (
        f_dec * (joined * b_dec + 1.0 - joined),
        f_state + joined * f_dec[..., None] * b_state,
        b_first,
        f_last,
    )
    return select_tree(b_first < 0, follow, select_tree(f_first < 0, before, merged))


def join_backward(before, follow):
    b_dec, b_state, b_first, b_last = before
    f_dec, f_state, f_first, f_last = follow
    joined = ((f_first == f_last) & (f_last == b_first)).astype(jnp.float32)
    merged = (
        f_dec * (joined * b_dec + 1.0 - joined),
        f_state + joined * f_dec[..., None] * b_state,
        f_first,
        b_last,
    )
    return select_tree(b_first < 0, follow, select_tree(f_first < 0, before, merged))


def join_sums(before, follow):
    b_sum, b_first, b_last = before
    f_sum, f_first, f_last = follow
    joined = ((f_first == f_last) & (f_last == b_first)).astype(jnp.float32)
    merged = (f_sum + joined * b_sum, f_first, b_last)
    return select_tree(b_first < 0, follow, select_tree(f_first < 0, before, merged))


def inverse_of(order_lists):
    block_count = order_lists.shape[-1]
    slot_ids = jnp.arange(block_count, dtype=jnp.int32)
    matches = order_lists[..., :, None] == slot_ids
    return jnp.sum(jnp.where(matches, slot_ids[:, None], 0), axis=-2)


def body(query_rows, key_rows, value_rows, log_decay, out_grad, doc_ids, block_order):
    dp_count = lax.axis_size("dp")
    dp_index = lax.axis_index("dp")
    row_count = query_rows.shape[1]
    block_count = row_count // BLK
    per_peer = block_count // dp_count
    order_lists = block_order[:, 0, :]
    my_order = order_lists[dp_index]
    gathered = (
        lax.all_gather(query_rows, "dp", axis=0, tiled=True),
        lax.all_gather(key_rows, "dp", axis=0, tiled=True),
        lax.all_gather(value_rows, "dp", axis=0, tiled=True),
        lax.all_gather(log_decay, "dp", axis=0, tiled=True),
    )
    inverse = inverse_of(order_lists)
    wanted = dp_index * per_peer + jnp.arange(per_peer, dtype=jnp.int32)
    slot_ids = inverse[:, wanted]
    source_ids = jnp.arange(dp_count, dtype=jnp.int32)[:, None]
    balanced = tuple(
        (
            whole.reshape(dp_count, block_count, BLK, whole.shape[-1])[
                source_ids, slot_ids
            ].reshape(row_count, whole.shape[-1])
            for whole in gathered
        )
    )
    query_bal, key_bal, value_bal, decay_bal = balanced
    doc_row = doc_ids[0]
    parts = prepare(query_bal, key_bal, value_bal, decay_bal, doc_row)
    head_count = parts["query_f"].shape[1]
    grad_f = out_grad[0].astype(jnp.float32).reshape(row_count, head_count, DV)
    first_f = parts["first_id"].astype(jnp.float32)
    last_f = parts["last_id"].astype(jnp.float32)
    neutral = (
        jnp.ones((head_count, DK), jnp.float32),
        jnp.zeros((head_count, DK, DV), jnp.float32),
        jnp.float32(-1.0),
        jnp.float32(-1.0),
    )
    unused_dec, state_in, unused_first, prior_last = prefix(
        (parts["decay_all"], state_end(parts), first_f, last_f), "ctx", join_forward, neutral, False
    )
    use_state = (prior_last == first_f).astype(jnp.float32)
    other_dec, carry_in, next_first, other_last = prefix(
        (parts["decay_all"], start_grad(parts, grad_f), first_f, last_f),
        "ctx",
        join_backward,
        neutral,
        True,
    )
    use_carry = (next_first == last_f).astype(jnp.float32)
    attn_rows, grad_query, grad_key, grad_value, grad_log, sum_start = finish(
        parts, grad_f, state_in, use_state, carry_in, use_carry
    )
    sums_in, later_first, later_last = prefix(
        (sum_start, first_f, last_f),
        "ctx",
        join_sums,
        (jnp.zeros((head_count, DK), jnp.float32), jnp.float32(-1.0), jnp.float32(-1.0)),
        True,
    )
    use_sums = (later_first == last_f).astype(jnp.float32)
    grad_decay = decay_grad_of(parts, grad_log, sums_in, use_sums)
    attn_out = attn_rows.reshape(row_count, head_count * DV).astype(jnp.bfloat16)[None]
    query_back = grad_query.reshape(row_count, head_count * DK).astype(jnp.bfloat16)
    key_back = grad_key.reshape(row_count, head_count * DK).astype(jnp.bfloat16)
    value_back = grad_value.reshape(row_count, head_count * DV).astype(jnp.bfloat16)
    decay_back = grad_decay.reshape(row_count, head_count * DK).astype(jnp.bfloat16)
    gathered_back = (
        lax.all_gather(query_back[None], "dp", axis=0, tiled=True),
        lax.all_gather(key_back[None], "dp", axis=0, tiled=True),
        lax.all_gather(value_back[None], "dp", axis=0, tiled=True),
        lax.all_gather(decay_back[None], "dp", axis=0, tiled=True),
    )
    dest_ids = my_order // per_peer
    dest_slots = dp_index * per_peer + my_order % per_peer
    returned = tuple(
        (
            whole.reshape(dp_count, block_count, BLK, whole.shape[-1])[
                dest_ids, dest_slots
            ].reshape(1, row_count, whole.shape[-1])
            for whole in gathered_back
        )
    )
    query_grad, key_grad, value_grad, decay_grad = returned
    return (attn_out, query_grad, key_grad, value_grad, decay_grad)


def solution(mesh):
    placed = (
        P("dp", "ctx", None),
        P("dp", "ctx", None),
        P("dp", "ctx", None),
        P("dp", "ctx", None),
        P("dp", "ctx", None),
        P("dp", "ctx"),
        P(None, "ctx", None),
    )
    return jax.shard_map(
        body,
        mesh=mesh,
        in_specs=placed,
        out_specs=(
            P("dp", "ctx", None),
            P("dp", "ctx", None),
            P("dp", "ctx", None),
            P("dp", "ctx", None),
            P("dp", "ctx", None),
        ),
        check_vma=False,
    )
```

profile of v0, /device:TPU:0, one launch (start us, length us, event | category | flops | bytes accessed | tf_op | source)
XLA Modules:
  0.0 467.1 jit_solution(8892131721895761153)
XLA Ops:
  15.5 23.7 %all-gather.18.cloned.1.call-done = bf16[4,128,1024]{2,1,0:T(8,128)(2,1)} async-done(((bf16[1,128,1024]{2,1,0:T(8,128)(2,1)}), bf16[4,128,1024]{2,1,0:T(8,128)(2,1)}) %all-gather.18.cloned.1.call-update) | async-done | bytes 1048592 | tf_op jit(solution)/shard_map/all_gather | solution.py:188
  44.1 23.6 %all-gather.16.cloned.1.call-done = bf16[4,128,1024]{2,1,0:T(8,128)(2,1)} async-done(((bf16[1,128,1024]{2,1,0:T(8,128)(2,1)}), bf16[4,128,1024]{2,1,0:T(8,128)(2,1)}) %all-gather.16.cloned.1.call-update) | async-done | bytes 1048592 | tf_op jit(solution)/shard_map/all_gather | solution.py:185
  74.6 21.7 %all-gather.20.cloned.1.call-done = bf16[4,128,1024]{2,1,0:T(8,128)(2,1)} async-done(((bf16[1,128,1024]{2,1,0:T(8,128)(2,1)}), bf16[4,128,1024]{2,1,0:T(8,128)(2,1)}) %all-gather.20.cloned.1.call-update) | async-done | bytes 1048592 | tf_op jit(solution)/shard_map/all_gather | solution.py:186
  101.6 31.6 %all-gather.14.cloned.1.call-done = bf16[4,128,2048]{2,1,0:T(8,128)(2,1)} async-done(((bf16[1,128,2048]{2,1,0:T(8,128)(2,1)}), bf16[4,128,2048]{2,1,0:T(8,128)(2,1)}) %all-gather.14.cloned.1.call-update) | async-done | bytes 2097168 | tf_op jit(solution)/shard_map/all_gather | solution.py:187
  133.3 2.2 gather_fusion
  140.4 17.0 %all-reduce.3 = (f32[8]{0:T(128)S(1)}, f32[8]{0:T(128)S(1)}) all-reduce(f32[8]{0:T(128)S(1)} %dynamic-update-slice.1, f32[8]{0:T(128)S(1)} %dynamic-update-slice.2), channel_id=1, replica_groups=mesh['dp'=4,'ctx'=8] {'ctx'}, use_global_device_ids=true, to_apply=%add.1 | all-reduce | flops 16 | bytes 128
  157.5 14.2 %all_gather.78 = f32[8,16,64]{2,1,0:T(8,128)S(1)} all-gather(f32[1,16,64]{2,1,0:T(8,128)S(1)} %get-tuple-element.421), channel_id=1, replica_groups=mesh['dp'=4,'ctx'=8] {'ctx'}, dimensions={0}, use_global_device_ids=true | all-gather | bytes 36864 | tf_op jit(solution)/shard_map/all_gather | solution.py:18
  173.2 9.4 %all-gather.32.cloned.1.call-done = f32[128,64,128]{2,1,0:T(8,128)} async-done(((f32[16,64,128]{2,1,0:T(8,128)}), f32[128,64,128]{2,1,0:T(8,128)}) %all-gather.32.cloned.1.call-update) | async-done | bytes 4194320 | tf_op jit(solution)/shard_map/all_gather | solution.py:18
  182.6 45.4 %while.51 = (s32[]{:T(128)}, f32[16,64,128]{2,1,0:T(8,128)S(1)}, f32[]{:T(128)}, s32[]{:T(128)}, f32[8,16,64,128]{3,2,1,0:T(8,128)}, /*index=5*/f32[8]{0:T(128)S...) while((s32[]{:T(128)}, f32[16,64,128]{2,1,0:T(8,128)S(1)}, ...), condition=%wide.region_5.6_spmd, body=%wide.region_4.5_spmd.sunk | while | flops 525326 | bytes 1585431 | solution.py:27
  228.0 2.5 all-gather.30.cloned.1.call-done
  233.7 2.2 fusion.12
  239.2 61.9 %all-gather.2 = f32[128,64]{1,0:T(8,128)S(1)} all-gather(f32[16,64]{1,0:T(8,128)S(1)} %get-tuple-element.419), channel_id=4, replica_groups=mesh['dp'=4,'ctx'=8] {'ctx'}, dimensions={0}, use_global_device_ids=true | all-gather | bytes 36864 | tf_op jit(solution)/shard_map/all_gather | solution.py:18
  301.0 34.3 %while.52 = (s32[]{:T(128)}, f32[16,64]{1,0:T(8,128)S(1)}, f32[]{:T(128)}, s32[]{:T(128)}, f32[8,16,64]{2,1,0:T(8,128)S(1)}, /*index=5*/f32[8]{0:T(128)S(1)}, f3...) while((s32[]{:T(128)}, f32[16,64]{1,0:T(8,128)S(1)}, f32[]{:T(128)}, ...), condition=%wide.region_8.9_spmd, body=%wide.region_7.8_spmd.sunk | while | flops 4110 | bytes 12555 | solution.py:27
  341.2 2.9 convolution_multiply_fusion.3
  346.1 2.8 fusion.9
  352.0 2.4 fusion.24
  357.3 5.4 %all-gather.28.cloned.1.call-done = bf16[4,128,1024]{2,1,0:T(8,128)(2,1)} async-done(((bf16[1,128,1024]{2,1,0:T(8,128)(2,1)}), bf16[4,128,1024]{2,1,0:T(8,128)(2,1)}) %all-gather.28.cloned.1.call-update) | async-done | bytes 1048592 | tf_op jit(solution)/shard_map/all_gather | solution.py:248
  362.6 2.5 gather_fusion.7
  365.1 26.0 %all-gather.24.cloned.1.call-done = bf16[4,128,1024]{2,1,0:T(8,128)(2,1)} async-done(((bf16[1,128,1024]{2,1,0:T(8,128)(2,1)}), bf16[4,128,1024]{2,1,0:T(8,128)(2,1)}) %all-gather.24.cloned.1.call-update) | async-done | bytes 1048592 | tf_op jit(solution)/shard_map/all_gather | solution.py:246
  391.1 2.5 gather_fusion.5
  393.6 26.6 %all-gather.22.cloned.1.call-done = bf16[4,128,1024]{2,1,0:T(8,128)(2,1)} async-done(((bf16[1,128,1024]{2,1,0:T(8,128)(2,1)}), bf16[4,128,1024]{2,1,0:T(8,128)(2,1)}) %all-gather.22.cloned.1.call-update) | async-done | bytes 1048592 | tf_op jit(solution)/shard_map/all_gather | solution.py:245
  420.2 2.5 gather_fusion.4
  422.7 34.5 %all-gather.26.cloned.1.call-done = bf16[4,128,2048]{2,1,0:T(8,128)(2,1)} async-done(((bf16[1,128,2048]{2,1,0:T(8,128)(2,1)}), bf16[4,128,2048]{2,1,0:T(8,128)(2,1)}) %all-gather.26.cloned.1.call-update) | async-done | bytes 2097168 | tf_op jit(solution)/shard_map/all_gather | solution.py:247
  457.3 3.0 gather_fusion.6
  (139 shorter events, 78.3 us)
Async XLA Ops:
  7.2 32.0 %all-gather.18.cloned.1.call-start = ((), (), s32[]{:S(2)}) async-start(), calls=%async_computation.2 | async-start | bytes 1310720 | tf_op jit(solution)/shard_map/all_gather | solution.py:188
  7.9 59.8 %all-gather.16.cloned.1.call-start = ((), (), s32[]{:S(2)}) async-start(), calls=%async_computation.1 | async-start | bytes 1310720 | tf_op jit(solution)/shard_map/all_gather | solution.py:185
  8.6 87.6 %all-gather.20.cloned.1.call-start = ((), (), s32[]{:S(2)}) async-start(), calls=%async_computation.3 | async-start | bytes 1310720 | tf_op jit(solution)/shard_map/all_gather | solution.py:186
  9.4 123.9 %all-gather.14.cloned.1.call-start = ((), (), s32[]{:S(2)}) async-start(), calls=%async_computation | async-start | bytes 2621440 | tf_op jit(solution)/shard_map/all_gather | solution.py:187
  10.0 172.6 %all-gather.32.cloned.1.call-start = ((), (), s32[]{:S(2)}) async-start(), calls=%async_computation.9 | async-start | bytes 4718592 | tf_op jit(solution)/shard_map/all_gather | solution.py:18
  43.7 25.8 %copy-start.7 = (f32[128,16,64]{2,1,0:T(8,128)}, f32[128,16,64]{2,1,0:T(8,128)S(1)}, u32[]{:S(2)}) copy-start(f32[128,16,64]{2,1,0:T(8,128)S(1)} %fusion.44) | copy-start | bytes 1572868
  72.4 25.6 %copy-start.5 = (f32[128,16,64]{0,2,1:T(8,128)}, f32[128,16,64]{0,2,1:T(8,128)S(1)}, u32[]{:S(2)}) copy-start(f32[128,16,64]{0,2,1:T(8,128)S(1)} %copy.125) | copy-start | bytes 1572868
  72.5 62.9 %copy-start = (f32[128,16,64]{0,2,1:T(8,128)}, f32[128,16,64]{0,2,1:T(8,128)S(1)}, u32[]{:S(2)}) copy-start(f32[128,16,64]{0,2,1:T(8,128)S(1)} %exponential_multiply_fusion) | copy-start | bytes 1572868
  74.5 63.8 %copy-start.9 = (u32[32]{0:T(128)S(1)}, u32[32]{0:T(128)}, u32[]{:S(2)}) copy-start(u32[32]{0:T(128)} %constant.302) | copy-start | bytes 388
  74.5 82.9 %copy-start.8 = (s32[1,128]{1,0:T(1,128)S(1)}, s32[1,128]{1,0:T(1,128)}, u32[]{:S(2)}) copy-start(s32[1,128]{1,0:T(1,128)} %param.18) | copy-start | bytes 1540
  74.5 156.0 %all-gather.30.cloned.1.call-start = ((), (), s32[]{:S(2)}) async-start(), calls=%async_computation.8 | async-start | bytes 4718592 | tf_op jit(solution)/shard_map/all_gather | solution.py:18
  137.1 225.6 %all-gather.28.cloned.1.call-start = ((), (), s32[]{:S(2)}) async-start(), calls=%async_computation.7 | async-start | bytes 1310720 | tf_op jit(solution)/shard_map/all_gather | solution.py:248
  230.6 3.1 copy-start.3
  230.6 5.2 %copy-start.1 = (f32[128,16,64]{0,2,1:T(8,128)S(1)}, f32[128,16,64]{0,2,1:T(8,128)}, u32[]{:S(2)}) copy-start(f32[128,16,64]{0,2,1:T(8,128)} %copy-done) | copy-start | bytes 1572868
  230.6 5.2 %copy-start.6 = (f32[128,16,64]{0,2,1:T(8,128)S(1)}, f32[128,16,64]{0,2,1:T(8,128)}, u32[]{:S(2)}) copy-start(f32[128,16,64]{0,2,1:T(8,128)} %copy-done.5) | copy-start | bytes 1572868
  337.4 53.7 %all-gather.24.cloned.1.call-start = ((), (), s32[]{:S(2)}) async-start(), calls=%async_computation.5 | async-start | bytes 1310720 | tf_op jit(solution)/shard_map/all_gather | solution.py:246
  339.3 80.9 %all-gather.22.cloned.1.call-start = ((), (), s32[]{:S(2)}) async-start(), calls=%async_computation.4 | async-start | bytes 1310720 | tf_op jit(solution)/shard_map/all_gather | solution.py:245
  341.2 116.1 %all-gather.26.cloned.1.call-start = ((), (), s32[]{:S(2)}) async-start(), calls=%async_computation.6 | async-start | bytes 2621440 | tf_op jit(solution)/shard_map/all_gather | solution.py:247
  344.1 1.0 copy-start.4
  346.1 8.3 %copy-start.2 = (f32[128,16,64]{0,2,1:T(8,128)S(1)}, f32[128,16,64]{0,2,1:T(8,128)}, u32[]{:S(2)}) copy-start(f32[128,16,64]{0,2,1:T(8,128)} %copy-done) | copy-start | bytes 1572868
Sparse Core Ops, SparseCore 0:
  9.8 29.3 all-gather.17
  41.0 26.6 all-gather.15
  69.6 26.6 all-gather.19
  97.9 35.2 all-gather.13
  134.7 47.8 all-gather.31
  184.6 45.8 all-gather.29
  337.6 25.0 all-gather.27
  364.5 26.6 all-gather.23
  393.6 26.6 all-gather.21
  421.9 35.2 all-gather.25
where the time goes:
time: 469 us; the launch traced here: 467 us
  waiting for transfers between devices  208 us (44%)
  blocking collectives  93 us (20%)
  local copies, waits for them, and re-layouts  57.1 us (12%)
  loops' own time  52.2 us (11%)
  matrix products  23.1 us (5%)
  other arithmetic  18 us (4%)
  between operations  15.7 us (3%)
    all_gather x2, blocking collectives, prefix(): gathered = jax.tree.map(lambda a: lax.all_gather(a, axis), part)  76 us
    another operation x3, loops' own time, prefix(): return lax.fori_loop(0, ahead, one, state)  52.2 us
    all_gather x1, waiting for transfers between devices, body(): lax.all_gather(value_back[None], 'dp', axis=0, tiled=True)  34.5 us
    all_gather x1, waiting for transfers between devices, body(): lax.all_gather(value_rows, 'dp', axis=0, tiled=True)  31.6 us
    all_gather x1, waiting for transfers between devices, body(): lax.all_gather(query_back[None], 'dp', axis=0, tiled=True)  26.6 us
    all_gather x1, waiting for transfers between devices, body(): lax.all_gather(key_back[None], 'dp', axis=0, tiled=True)  26 us
    all_gather x1, waiting for transfers between devices, body(): lax.all_gather(log_decay, 'dp', axis=0, tiled=True)  23.7 us
    all_gather x1, waiting for transfers between devices, body(): lax.all_gather(query_rows, 'dp', axis=0, tiled=True)  23.6 us
  transfers between devices with their start and end apart: 10, of which 10 were waited for; matrix products, arithmetic and copies ran while one was open for 16% of the time, Pallas kernels for 0%

commit v1 on v0

v1 whole, which is shorter than its diff:
```python
import functools

import jax
import jax.numpy as jnp
from jax import lax
from jax.experimental import pallas as pl
from jax.experimental.pallas import tpu as pltpu
from jax.sharding import PartitionSpec as P

DK = 64
DV = 128
BLK = 32
KW = 2 * DK
VW = 2 * DV
W = 3 * KW + VW
MESH = pl.DeviceIdType.MESH
F32 = jnp.float32
BF16 = jnp.bfloat16

NN = (((1,), (0,)), ((), ()))
NT = (((1,), (1,)), ((), ()))
TN = (((0,), (0,)), ((), ()))


def split(x):
    hi = x.astype(BF16)
    return hi, (x - hi.astype(F32)).astype(BF16)


def dot(a, b, dims):
    a = a if isinstance(a, tuple) else (a,)
    b = b if isinstance(b, tuple) else (b,)
    total = None
    for i, left in enumerate(a):
        for j, right in enumerate(b):
            if i + j > 1:
                continue
            term = lax.dot_general(left, right, dims, preferred_element_type=F32)
            total = term if total is None else total + term
    return total


def both(fn, pair):
    return tuple(fn(x) for x in pair)


def kernel(
    n_dp, n_ctx, order_ref, doc_ref, q_ref, k_ref, v_ref, d_ref, g_ref,
    out_ref, dq_ref, dk_ref, dv_ref, dd_ref,
    sx, rx, sy, ry, f_own, f_in, b_own, b_in, doc_prev, doc_next,
    x_send, x_recv, y_send, y_recv, f_send, f_recv, b_send, b_recv, doc_send, doc_recv,
):
    me = lax.axis_index("dp")
    pos = lax.axis_index("ctx")
    rows = q_ref.shape[1]
    pairs = q_ref.shape[2] // KW
    blocks = rows // BLK
    per = blocks // n_dp
    part = per * BLK
    has_prev = pos > 0
    has_next = pos < n_ctx - 1

    barrier = pltpu.get_barrier_semaphore()
    for r in range(1, n_dp):
        peer = lax.rem(me + r, n_dp)
        pl.semaphore_signal(barrier, inc=1, device_id={"dp": peer}, device_id_type=MESH)

    @pl.when(has_prev)
    def _():
        pl.semaphore_signal(barrier, inc=1, device_id={"ctx": pos - 1}, device_id_type=MESH)

    @pl.when(has_next)
    def _():
        pl.semaphore_signal(barrier, inc=1, device_id={"ctx": pos + 1}, device_id_type=MESH)

    def my_rows(index):
        return pl.ds(pl.multiple_of(index * part, part), part)

    def lanes(h, width):
        return pl.ds(pl.multiple_of(h * width, width), width)

    order = [order_ref[me, 0, j] for j in range(blocks)]

    def piece(j):
        return slice(j * BLK, (j + 1) * BLK)

    def stage(h, carry):
        for src, width, at in ((q_ref, KW, 0), (k_ref, KW, KW), (d_ref, KW, 2 * KW), (v_ref, VW, 3 * KW)):
            parts = [src[0, piece(j), lanes(h, width)] for j in range(blocks)]
            for dest in range(blocks):
                chosen = parts[0]
                for j in range(1, blocks):
                    chosen = lax.select(order[j] == dest, parts[j], chosen)
                sx[h, piece(dest), at : at + width] = chosen
        rx[h, my_rows(me), :] = sx[h, my_rows(me), :]
        return carry

    lax.fori_loop(0, pairs, stage, 0)

    @pl.when(jnp.logical_not(has_prev))
    def _():
        doc_prev[...] = jnp.full_like(doc_prev, -1)
        f_in[...] = jnp.zeros_like(f_in)

    @pl.when(jnp.logical_not(has_next))
    def _():
        doc_next[...] = jnp.full_like(doc_next, -1)
        b_in[...] = jnp.zeros_like(b_in)

    peers = n_dp - 1 + has_prev.astype(jnp.int32) + has_next.astype(jnp.int32)
    pl.semaphore_wait(barrier, peers)

    def exchange(src, dst, send, recv, h, r):
        peer = lax.rem(me + r, n_dp)
        return pltpu.make_async_remote_copy(
            src_ref=src.at[h, my_rows(peer), :],
            dst_ref=dst.at[h, my_rows(me), :],
            send_sem=send.at[h, r],
            recv_sem=recv.at[h, r],
            device_id={"dp": peer},
            device_id_type=MESH,
        )

    def arrival(src, dst, send, recv, h, r):
        source = lax.rem(me + n_dp - r, n_dp)
        return pltpu.make_async_remote_copy(
            src_ref=src.at[h, my_rows(source), :],
            dst_ref=dst.at[h, my_rows(source), :],
            send_sem=send.at[h, r],
            recv_sem=recv.at[h, r],
            device_id={"dp": source},
            device_id_type=MESH,
        )

    def neighbour(src, dst, send, recv, step):
        return pltpu.make_async_remote_copy(
            src_ref=src, dst_ref=dst, send_sem=send, recv_sem=recv,
            device_id={"ctx": pos + step}, device_id_type=MESH,
        )

    def doc_up():
        return neighbour(doc_ref, doc_prev, doc_send.at[0], doc_recv.at[0], 1)

    def doc_down():
        return neighbour(doc_ref, doc_next, doc_send.at[1], doc_recv.at[1], -1)

    def chain_up(h):
        return neighbour(f_own.at[h], f_in.at[h], f_send.at[h], f_recv.at[h], 1)

    def chain_down(h):
        return neighbour(b_own.at[h], b_in.at[h], b_send.at[h], b_recv.at[h], -1)

    @pl.when(has_next)
    def _():
        doc_up().start()

    @pl.when(has_prev)
    def _():
        doc_down().start()

    def send_rows(h, carry):
        for r in range(1, n_dp):
            exchange(sx, rx, x_send, x_recv, h, r).start()
        return carry

    lax.fori_loop(0, pairs, send_rows, 0)

    @pl.when(has_prev)
    def _():
        doc_up().wait_recv()

    @pl.when(has_next)
    def _():
        doc_down().wait_recv()

    doc_row = jnp.broadcast_to(doc_ref[...].astype(F32), (rows, rows))
    doc_col = doc_row.T
    first_row = doc_col[0:1, :]
    last_row = doc_col[rows - 1 : rows, :]
    prev_last = jnp.broadcast_to(doc_prev[:, rows - 1 : rows].astype(F32), (1, rows))
    next_first = jnp.broadcast_to(doc_next[:, 0:1].astype(F32), (1, rows))
    use_state = (prev_last == first_row).astype(F32)
    use_carry = (next_first == last_row).astype(F32)
    single = (first_row == last_row).astype(F32)
    pass_state = single * use_state
    pass_carry = single * use_carry
    in_first = (doc_col == first_row).astype(F32)
    in_last = (doc_col == last_row).astype(F32)
    head_w = in_first * use_state
    tail_w = in_last * use_carry
    row_id = lax.broadcasted_iota(jnp.int32, (rows, rows), 0)
    lane_id = lax.broadcasted_iota(jnp.int32, (rows, rows), 1)
    same = (doc_row == doc_col) & (row_id >= lane_id)
    later = ((doc_row == doc_col) & (row_id <= lane_id)).astype(BF16)
    lower = (row_id >= lane_id).astype(BF16)
    in_a = lax.broadcasted_iota(jnp.int32, (rows, KW), 1) < DK
    factor = DK ** (-0.5)

    def load(h):
        q = rx[h, :, 0:KW]
        k = rx[h, :, KW : 2 * KW]
        d = rx[h, :, 2 * KW : 3 * KW]
        v = rx[h, :, 3 * KW : W]
        g = g_ref[0, :, lanes(h, VW)]
        cum = dot(lower, d, NN)
        total = cum[rows - 1 : rows, :]
        growth = jnp.exp(cum)
        shrink = jnp.exp(-cum)
        to_end = jnp.exp(total - cum)
        q_f = q.astype(F32)
        k_f = k.astype(F32)
        return q_f, k_f, v, g, d, growth, shrink, to_end

    def fold(wide):
        return jnp.concatenate([wide[0:DK, 0:DV], wide[DK:KW, DV:VW]], axis=0)

    def spread(tall):
        nil = jnp.zeros((DK, DV), tall.dtype)
        top = jnp.concatenate([tall[0:DK], nil], axis=1)
        low = jnp.concatenate([nil, tall[DK:KW]], axis=1)
        return jnp.concatenate([top, low], axis=0)

    def local(h, carry):
        for r in range(1, n_dp):
            arrival(sx, rx, x_send, x_recv, h, r).wait_recv()
        q_f, k_f, v, g, d, growth, shrink, to_end = load(h)
        f_own[h] = fold(dot(split(k_f * to_end * in_last), v, TN))
        b_own[h] = factor * fold(dot(split(q_f * growth * in_first), g, TN))
        return carry

    lax.fori_loop(0, pairs, local, 0)

    def decay_of(h):
        d = rx[h, :, 2 * KW : 3 * KW]
        return jnp.exp(dot(d, jnp.ones((rows, DV), BF16), TN))

    def finish(h):
        q_f, k_f, v, g, d, growth, shrink, to_end = load(h)
        q_t = q_f * growth
        k_t = k_f * shrink
        k_e = k_f * to_end * tail_w
        zero = jnp.zeros_like(q_t)
        q_2 = split(jnp.concatenate([jnp.where(in_a, q_t, zero), jnp.where(in_a, zero, q_t)], axis=0))
        k_s = split(k_t)
        k_2 = split(jnp.concatenate([jnp.where(in_a, k_t, zero), jnp.where(in_a, zero, k_t)], axis=0))
        same_2 = jnp.concatenate([same, same], axis=0)
        score_2 = split(jnp.where(same_2, dot(q_2, k_s, NT), 0.0))
        v_a, v_b = v[:, 0:DV], v[:, DV:VW]
        g_a, g_b = g[:, 0:DV], g[:, DV:VW]
        score_a = both(lambda x: x[0:rows], score_2)
        score_b = both(lambda x: x[rows : 2 * rows], score_2)
        state = both(spread, split(f_in[h]))
        carry = both(spread, split(b_in[h]))
        near = jnp.concatenate([dot(score_a, v_a, NN), dot(score_b, v_b, NN)], axis=1)
        far = dot(split(q_t * head_w), state, NN)
        out_ref[0, :, lanes(h, VW)] = (factor * (near + far)).astype(BF16)
        gs_a = jnp.where(same, dot(g_a, v_a, NT), 0.0)
        gs_b = jnp.where(same, dot(g_b, v_b, NT), 0.0)
        dq_near = dot(split(jnp.concatenate([gs_a, gs_b], axis=1)), k_2, NN)
        dq = factor * growth * (dq_near + dot(g, state, NT) * head_w)
        dk_near = dot(split(jnp.concatenate([gs_a, gs_b], axis=0)), q_2, TN)
        dk = factor * shrink * dk_near + to_end * dot(v, carry, NT) * tail_w
        dv_near = jnp.concatenate([dot(score_a, g_a, TN), dot(score_b, g_b, TN)], axis=1)
        dv = factor * dv_near + dot(split(k_e), carry, NN)
        log_grad = q_f * dq - k_f * dk
        sums = dot(jnp.ones((8, DV), BF16), split(f_own[h] * b_in[h]), NT)
        dd = dot(later, split(log_grad), NN) + sums[0:1] * tail_w
        sy[h, :, 0:KW] = dq.astype(BF16)
        sy[h, :, KW : 2 * KW] = dk.astype(BF16)
        sy[h, :, 2 * KW : 3 * KW] = dd.astype(BF16)
        sy[h, :, 3 * KW : W] = dv.astype(BF16)
        ry[h, my_rows(me), :] = sy[h, my_rows(me), :]
        for r in range(1, n_dp):
            exchange(sy, ry, y_send, y_recv, h, r).start()

    below = n_ctx - 1 - pos
    last_of = jnp.maximum(pos, below)

    def step(t, carry):
        up = t - pos
        down = t - below
        ready = t - last_of

        @pl.when((up >= 0) & (up < pairs))
        def _():
            @pl.when(has_prev)
            def _():
                chain_up(up).wait_recv()

            f_own[up] = f_own[up] + pass_state * decay_of(up) * f_in[up]

            @pl.when(has_next)
            def _():
                chain_up(up).start()

        @pl.when((down >= 0) & (down < pairs))
        def _():
            @pl.when(has_next)
            def _():
                chain_down(down).wait_recv()

            b_own[down] = b_own[down] + pass_carry * decay_of(down) * b_in[down]

            @pl.when(has_prev)
            def _():
                chain_down(down).start()

        @pl.when((ready >= 0) & (ready < pairs))
        def _():
            finish(ready)

        return carry

    lax.fori_loop(0, n_ctx - 1 + pairs, step, 0)

    def wait_back(h, carry):
        for r in range(1, n_dp):
            arrival(sy, ry, y_send, y_recv, h, r).wait_recv()
        return carry

    lax.fori_loop(0, pairs, wait_back, 0)

    def unpack(h, carry):
        for dst, width, at in ((dq_ref, KW, 0), (dk_ref, KW, KW), (dd_ref, KW, 2 * KW), (dv_ref, VW, 3 * KW)):
            parts = [ry[h, piece(j), at : at + width] for j in range(blocks)]
            for j in range(blocks):
                chosen = parts[0]
                for place in range(1, blocks):
                    chosen = lax.select(order[j] == place, parts[place], chosen)
                dst[0, piece(j), lanes(h, width)] = chosen
        return carry

    lax.fori_loop(0, pairs, unpack, 0)

    def drain(h, carry):
        for r in range(1, n_dp):
            exchange(sx, rx, x_send, x_recv, h, r).wait_send()
            exchange(sy, ry, y_send, y_recv, h, r).wait_send()

        @pl.when(has_next)
        def _():
            chain_up(h).wait_send()

        @pl.when(has_prev)
        def _():
            chain_down(h).wait_send()

        return carry

    lax.fori_loop(0, pairs, drain, 0)

    @pl.when(has_next)
    def _():
        doc_up().wait_send()

    @pl.when(has_prev)
    def _():
        doc_down().wait_send()


def body(n_dp, n_ctx, query_rows, key_rows, value_rows, log_decay, out_grad, doc_ids, block_order):
    rows, hk = query_rows.shape[1:]
    hv = value_rows.shape[2]
    pairs = hk // KW
    vmem = pl.BlockSpec(memory_space=pltpu.VMEM)
    keys = jax.ShapeDtypeStruct((1, rows, hk), BF16)
    values = jax.ShapeDtypeStruct((1, rows, hv), BF16)
    dma = pltpu.SemaphoreType.DMA
    out, dq, dk, dv, dd = pl.pallas_call(
        functools.partial(kernel, n_dp, n_ctx),
        out_shape=(values, keys, keys, values, keys),
        in_specs=[pl.BlockSpec(memory_space=pltpu.SMEM)] + [vmem] * 6,
        out_specs=(vmem,) * 5,
        scratch_shapes=[
            pltpu.VMEM((pairs, rows, W), BF16),
            pltpu.VMEM((pairs, rows, W), BF16),
            pltpu.VMEM((pairs, rows, W), BF16),
            pltpu.VMEM((pairs, rows, W), BF16),
            pltpu.VMEM((pairs, KW, DV), F32),
            pltpu.VMEM((pairs, KW, DV), F32),
            pltpu.VMEM((pairs, KW, DV), F32),
            pltpu.VMEM((pairs, KW, DV), F32),
            pltpu.VMEM((1, rows), jnp.int32),
            pltpu.VMEM((1, rows), jnp.int32),
            dma((pairs, n_dp)), dma((pairs, n_dp)), dma((pairs, n_dp)), dma((pairs, n_dp)),
            dma((pairs,)), dma((pairs,)), dma((pairs,)), dma((pairs,)),
            dma((2,)), dma((2,)),
        ],
        compiler_params=pltpu.CompilerParams(
            collective_id=0, has_side_effects=True, vmem_limit_bytes=40 * 1024 * 1024
        ),
    )(block_order, doc_ids, query_rows, key_rows, value_rows, log_decay, out_grad)
    return out, dq, dk, dv, dd


def solution(mesh):
    placed = P("dp", "ctx", None)
    return jax.shard_map(
        functools.partial(body, mesh.shape["dp"], mesh.shape["ctx"]),
        mesh=mesh,
        in_specs=(placed,) * 5 + (P("dp", "ctx"), P(None, "ctx", None)),
        out_specs=(placed,) * 5,
        check_vma=False,
    )
```

time: 469 us -> 71.5 us (0.15)
  waiting for transfers between devices: 208 us -> 0 us
  blocking collectives: 93 us -> 0 us
  Pallas kernels: 0 us -> 60.6 us
  loops' own time: 52.2 us -> 0 us
  local copies, waits for them, and re-layouts: 57.1 us -> 9.95 us
  matrix products: 23.1 us -> 0 us
  other arithmetic: 18 us -> 0 us
  between operations: 15.7 us -> 0.66 us
    all_gather x10 -> x0, waiting for transfers between devices: 205 us -> none  [the longest x1 34.5 us: body(): lax.all_gather(value_back[None], 'dp', axis=0, tiled=True)]
    all_gather x2 -> x0, blocking collectives: 76 us -> none  [prefix(): gathered = jax.tree.map(lambda a: lax.all_gather(a, axis), part)]
    pallas_call x0 -> x1, Pallas kernels: none -> 60.6 us  [body(): pl.pallas_call(functools.partial(kernel, n_dp, n_ctx), out_shape=(values,...]
    another operation x3 -> x0, loops' own time: 52.2 us -> none  [prefix(): return lax.fori_loop(0, ahead, one, state)]
    dot_general x12 -> x0, matrix products: 21.8 us -> none  [the longest x1 2.86 us: prepare(): jnp.einsum('thi,shi->hts', query_t, key_t, precision=HIGH) * same_doc[None]]
    gather x8 -> x0, local copies, waits for them, and re-layouts: 18 us -> none  [body(): whole.reshape(dp_count, block_count, BLK, whole.shape[-1])]
    unnamed x1 -> x0, blocking collectives: 17 us -> none
    dynamic_slice x28 -> x0, local copies, waits for them, and re-layouts: 16.9 us -> none  [one(): lax.dynamic_index_in_dim(a, source, 0, False)]
  transfers between devices with their start and end apart: 10 -> 0, of which waited for: 10 -> 0; matrix products, arithmetic and copies ran while one was open for 16% -> 0% of each run, Pallas kernels for 0% -> 0%
where the time goes in v1:
time: 71.5 us; the launch traced here: 71.2 us
  Pallas kernels  60.6 us (85%)
  local copies, waits for them, and re-layouts  9.95 us (14%)
    pallas_call x1, Pallas kernels, body(): pl.pallas_call(functools.partial(kernel, n_dp, n_ctx), out_shape=(values,...  60.6 us
    unnamed x19, local copies, waits for them, and re-layouts  9.95 us

profile of v1, /device:TPU:0, one launch (start us, length us, event | category | flops | bytes accessed | tf_op | source)
XLA Modules:
  0.0 71.2 jit_solution(6714572615581098670)
XLA Ops:
  0.6 0.0 copy-start
  0.6 1.0 %copy-done = bf16[1,128,2048]{2,1,0:T(8,128)(2,1)S(1)} copy-done((bf16[1,128,2048]{2,1,0:T(8,128)(2,1)S(1)}, bf16[1,128,2048]{2,1,0:T(8,128)(2,1)}, u32[]{:S(2)}) %copy-start) | copy-done | bytes 524312
  1.7 0.0 copy-start.1
  1.7 1.0 %copy-done.1 = bf16[1,128,2048]{2,1,0:T(8,128)(2,1)S(1)} copy-done((bf16[1,128,2048]{2,1,0:T(8,128)(2,1)S(1)}, bf16[1,128,2048]{2,1,0:T(8,128)(2,1)}, u32[]{:S(2)}) %copy-start.1) | copy-done | bytes 524312
  2.7 0.0 copy-start.2
  2.7 0.9 %copy-done.2 = bf16[1,128,1024]{2,1,0:T(8,128)(2,1)S(1)} copy-done((bf16[1,128,1024]{2,1,0:T(8,128)(2,1)S(1)}, bf16[1,128,1024]{2,1,0:T(8,128)(2,1)}, u32[]{:S(2)}) %copy-start.2) | copy-done | bytes 262168
  3.7 0.0 copy-start.3
  3.7 0.9 %copy-done.3 = bf16[1,128,1024]{2,1,0:T(8,128)(2,1)S(1)} copy-done((bf16[1,128,1024]{2,1,0:T(8,128)(2,1)S(1)}, bf16[1,128,1024]{2,1,0:T(8,128)(2,1)}, u32[]{:S(2)}) %copy-start.3) | copy-done | bytes 262168
  4.6 0.0 copy-start.4
  4.6 0.9 %copy-done.4 = bf16[1,128,1024]{2,1,0:T(8,128)(2,1)S(1)} copy-done((bf16[1,128,1024]{2,1,0:T(8,128)(2,1)S(1)}, bf16[1,128,1024]{2,1,0:T(8,128)(2,1)}, u32[]{:S(2)}) %copy-start.4) | copy-done | bytes 262168
  5.6 0.0 copy-start.5
  5.6 0.7 copy-done.5
  6.3 0.0 copy-start.6
  6.3 0.7 copy-done.6
  6.9 60.6 %shard_map.110 = (bf16[1,128,2048]{2,1,0:T(8,128)(2,1)S(1)}, bf16[1,128,1024]{2,1,0:T(8,128)(2,1)S(1)}, bf16[1,128,1024]{2,1,0:T(8,128)(2,1)S(1)}, bf16[1,128,20...) custom-call(s32[4,1,4]{2,1,0:T(1,128)S(1)} %copy-done.5, s32[1,128]{1,0:T(1,128)S(1)} %copy-done.6, ...), custom_call_target="tpu_custom_call" | custom-call | tf_op jit(solution)/shard_map/pallas_call | solution.py:369
  67.5 0.8 %copy.17 = bf16[1,128,2048]{2,1,0:T(8,128)(2,1)} copy(bf16[1,128,2048]{2,1,0:T(8,128)(2,1)S(1)} %get-tuple-element.10) | data formatting | bytes 1048576
  68.3 0.7 copy.18
  69.0 0.7 copy.19
  69.7 0.8 %copy.20 = bf16[1,128,2048]{2,1,0:T(8,128)(2,1)} copy(bf16[1,128,2048]{2,1,0:T(8,128)(2,1)S(1)} %get-tuple-element.13) | data formatting | bytes 1048576
  70.5 0.7 copy.21
Async XLA Ops:
  0.6 1.0 %copy-start = (bf16[1,128,2048]{2,1,0:T(8,128)(2,1)S(1)}, bf16[1,128,2048]{2,1,0:T(8,128)(2,1)}, u32[]{:S(2)}) copy-start(bf16[1,128,2048]{2,1,0:T(8,128)(2,1)} %v_ref.1) | copy-start | bytes 1572868
  1.7 1.0 %copy-start.1 = (bf16[1,128,2048]{2,1,0:T(8,128)(2,1)S(1)}, bf16[1,128,2048]{2,1,0:T(8,128)(2,1)}, u32[]{:S(2)}) copy-start(bf16[1,128,2048]{2,1,0:T(8,128)(2,1)} %g_ref.1) | copy-start | bytes 1572868
  2.7 0.9 %copy-start.2 = (bf16[1,128,1024]{2,1,0:T(8,128)(2,1)S(1)}, bf16[1,128,1024]{2,1,0:T(8,128)(2,1)}, u32[]{:S(2)}) copy-start(bf16[1,128,1024]{2,1,0:T(8,128)(2,1)} %q_ref.1) | copy-start | bytes 786436
  3.7 0.9 %copy-start.3 = (bf16[1,128,1024]{2,1,0:T(8,128)(2,1)S(1)}, bf16[1,128,1024]{2,1,0:T(8,128)(2,1)}, u32[]{:S(2)}) copy-start(bf16[1,128,1024]{2,1,0:T(8,128)(2,1)} %k_ref.1) | copy-start | bytes 786436
  4.6 0.9 %copy-start.4 = (bf16[1,128,1024]{2,1,0:T(8,128)(2,1)S(1)}, bf16[1,128,1024]{2,1,0:T(8,128)(2,1)}, u32[]{:S(2)}) copy-start(bf16[1,128,1024]{2,1,0:T(8,128)(2,1)} %d_ref.1) | copy-start | bytes 786436
  5.6 0.7 copy-start.5
  6.3 0.7 copy-start.6

commit v2 on v1

--- a/solution.py
+++ b/solution.py
@@ -45,15 +45,16 @@
 
 
 def kernel(
-    n_dp, n_ctx, order_ref, doc_ref, q_ref, k_ref, v_ref, d_ref, g_ref,
+    n_dp, n_ctx, order_hbm, doc_hbm, q_hbm, k_hbm, v_hbm, d_hbm, g_hbm,
     out_ref, dq_ref, dk_ref, dv_ref, dd_ref,
+    order_ref, doc_ref, q_ref, k_ref, v_ref, d_ref, g_ref, in_sem, decay,
     sx, rx, sy, ry, f_own, f_in, b_own, b_in, doc_prev, doc_next,
     x_send, x_recv, y_send, y_recv, f_send, f_recv, b_send, b_recv, doc_send, doc_recv,
 ):
     me = lax.axis_index("dp")
     pos = lax.axis_index("ctx")
-    rows = q_ref.shape[1]
-    pairs = q_ref.shape[2] // KW
+    rows = q_hbm.shape[1]
+    pairs = q_hbm.shape[2] // KW
     blocks = rows // BLK
     per = blocks // n_dp
     part = per * BLK
@@ -73,29 +74,24 @@
     def _():
         pl.semaphore_signal(barrier, inc=1, device_id={"ctx": pos + 1}, device_id_type=MESH)
 
+    fetches = [
+        pltpu.make_async_copy(src, dst, in_sem.at[i])
+        for i, (src, dst) in enumerate((
+            (order_hbm, order_ref), (q_hbm, q_ref), (k_hbm, k_ref), (d_hbm, d_ref),
+            (v_hbm, v_ref), (doc_hbm, doc_ref), (g_hbm, g_ref),
+        ))
+    ]
+    for fetch in fetches:
+        fetch.start()
+
     def my_rows(index):
         return pl.ds(pl.multiple_of(index * part, part), part)
 
     def lanes(h, width):
         return pl.ds(pl.multiple_of(h * width, width), width)
 
-    order = [order_ref[me, 0, j] for j in range(blocks)]
-
-    def piece(j):
-        return slice(j * BLK, (j + 1) * BLK)
-
-    def stage(h, carry):
-        for src, width, at in ((q_ref, KW, 0), (k_ref, KW, KW), (d_ref, KW, 2 * KW), (v_ref, VW, 3 * KW)):
-            parts = [src[0, piece(j), lanes(h, width)] for j in range(blocks)]
-            for dest in range(blocks):
-                chosen = parts[0]
-                for j in range(1, blocks):
-                    chosen = lax.select(order[j] == dest, parts[j], chosen)
-                sx[h, piece(dest), at : at + width] = chosen
-        rx[h, my_rows(me), :] = sx[h, my_rows(me), :]
-        return carry
-
-    lax.fori_loop(0, pairs, stage, 0)
+    for fetch in fetches[:5]:
+        fetch.wait()
 
     @pl.when(jnp.logical_not(has_prev))
     def _():
@@ -150,20 +146,36 @@
     def chain_down(h):
         return neighbour(b_own.at[h], b_in.at[h], b_send.at[h], b_recv.at[h], -1)
 
-    @pl.when(has_next)
-    def _():
-        doc_up().start()
-
-    @pl.when(has_prev)
-    def _():
-        doc_down().start()
-
-    def send_rows(h, carry):
+    order = [order_ref[me, 0, j] for j in range(blocks)]
+
+    def piece(j):
+        return slice(j * BLK, (j + 1) * BLK)
+
+    def stage(h, carry):
+        for src, width, at in ((q_ref, KW, 0), (k_ref, KW, KW), (d_ref, KW, 2 * KW), (v_ref, VW, 3 * KW)):
+            parts = [src[0, piece(j), lanes(h, width)] for j in range(blocks)]
+            for dest in range(blocks):
+                chosen = parts[0]
+                for j in range(1, blocks):
+                    chosen = lax.select(order[j] == dest, parts[j], chosen)
+                sx[h, piece(dest), at : at + width] = chosen
+        rx[h, my_rows(me), :] = sx[h, my_rows(me), :]
         for r in range(1, n_dp):
             exchange(sx, rx, x_send, x_recv, h, r).start()
         return carry
 
-    lax.fori_loop(0, pairs, send_rows, 0)
+    lax.fori_loop(0, pairs, stage, 0)
+
+    for fetch in fetches[5:]:
+        fetch.wait()
+
+    @pl.when(has_next)
+    def _():
+        doc_up().start()
+
+    @pl.when(has_prev)
+    def _():
+        doc_down().start()
 
     @pl.when(has_prev)
     def _():
@@ -220,19 +232,13 @@
         low = jnp.concatenate([nil, tall[DK:KW]], axis=1)
         return jnp.concatenate([top, low], axis=0)
 
-    def local(h, carry):
+    def local(h):
         for r in range(1, n_dp):
             arrival(sx, rx, x_send, x_recv, h, r).wait_recv()
         q_f, k_f, v, g, d, growth, shrink, to_end = load(h)
         f_own[h] = fold(dot(split(k_f * to_end * in_last), v, TN))
         b_own[h] = factor * fold(dot(split(q_f * growth * in_first), g, TN))
-        return carry
-
-    lax.fori_loop(0, pairs, local, 0)
-
-    def decay_of(h):
-        d = rx[h, :, 2 * KW : 3 * KW]
-        return jnp.exp(dot(d, jnp.ones((rows, DV), BF16), TN))
+        decay[h] = jnp.exp(dot(d, jnp.ones((rows, DV), BF16), TN))
 
     def finish(h):
         q_f, k_f, v, g, d, growth, shrink, to_end = load(h)
@@ -277,9 +283,9 @@
     last_of = jnp.maximum(pos, below)
 
     def step(t, carry):
-        up = t - pos
-        down = t - below
-        ready = t - last_of
+        up = t - 1 - pos
+        down = t - 1 - below
+        ready = t - 1 - last_of
 
         @pl.when((up >= 0) & (up < pairs))
         def _():
@@ -287,7 +293,7 @@
             def _():
                 chain_up(up).wait_recv()
 
-            f_own[up] = f_own[up] + pass_state * decay_of(up) * f_in[up]
+            f_own[up] = f_own[up] + pass_state * decay[up] * f_in[up]
 
             @pl.when(has_next)
             def _():
@@ -299,19 +305,23 @@
             def _():
                 chain_down(down).wait_recv()
 
-            b_own[down] = b_own[down] + pass_carry * decay_of(down) * b_in[down]
+            b_own[down] = b_own[down] + pass_carry * decay[down] * b_in[down]
 
             @pl.when(has_prev)
             def _():
                 chain_down(down).start()
 
+        @pl.when(t < pairs)
+        def _():
+            local(t)
+
         @pl.when((ready >= 0) & (ready < pairs))
         def _():
             finish(ready)
 
         return carry
 
-    lax.fori_loop(0, n_ctx - 1 + pairs, step, 0)
+    lax.fori_loop(0, n_ctx + pairs, step, 0)
 
     def wait_back(h, carry):
         for r in range(1, n_dp):
@@ -369,9 +379,18 @@
     out, dq, dk, dv, dd = pl.pallas_call(
         functools.partial(kernel, n_dp, n_ctx),
         out_shape=(values, keys, keys, values, keys),
-        in_specs=[pl.BlockSpec(memory_space=pltpu.SMEM)] + [vmem] * 6,
+        in_specs=[pl.BlockSpec(memory_space=pltpu.HBM)] * 7,
         out_specs=(vmem,) * 5,
         scratch_shapes=[
+            pltpu.SMEM(block_order.shape, jnp.int32),
+            pltpu.VMEM((1, rows), jnp.int32),
+            pltpu.VMEM((1, rows, hk), BF16),
+            pltpu.VMEM((1, rows, hk), BF16),
+            pltpu.VMEM((1, rows, hv), BF16),
+            pltpu.VMEM((1, rows, hk), BF16),
+            pltpu.VMEM((1, rows, hv), BF16),
+            dma((7,)),
+            pltpu.VMEM((pairs, KW, DV), F32),
             pltpu.VMEM((pairs, rows, W), BF16),
             pltpu.VMEM((pairs, rows, W), BF16),
             pltpu.VMEM((pairs, rows, W), BF16),

time: 71.5 us -> 59.1 us (0.83)
  Pallas kernels: 60.6 us -> 48.1 us
    pallas_call x1, Pallas kernels: 60.6 us -> 48.1 us  [body(): pl.pallas_call(functools.partial(kernel, n_dp, n_ctx), out_shape=(values,...]
where the time goes in v2:
time: 59.1 us; the launch traced here: 58.7 us
  Pallas kernels  48.1 us (81%)
  local copies, waits for them, and re-layouts  9.95 us (17%)
  between operations  0.66 us (1%)
    pallas_call x1, Pallas kernels, body(): pl.pallas_call(functools.partial(kernel, n_dp, n_ctx), out_shape=(values,...  48.1 us
    unnamed x19, local copies, waits for them, and re-layouts  9.95 us

profile of v2, /device:TPU:0, one launch (start us, length us, event | category | flops | bytes accessed | tf_op | source)
XLA Modules:
  0.0 58.7 jit_solution(1306407901276357106)
XLA Ops:
  0.6 0.0 copy-start
  0.6 1.0 %copy-done = bf16[1,128,2048]{2,1,0:T(8,128)(2,1)S(1)} copy-done((bf16[1,128,2048]{2,1,0:T(8,128)(2,1)S(1)}, bf16[1,128,2048]{2,1,0:T(8,128)(2,1)}, u32[]{:S(2)}) %copy-start) | copy-done | bytes 524312
  1.7 0.0 copy-start.1
  1.7 1.0 %copy-done.1 = bf16[1,128,2048]{2,1,0:T(8,128)(2,1)S(1)} copy-done((bf16[1,128,2048]{2,1,0:T(8,128)(2,1)S(1)}, bf16[1,128,2048]{2,1,0:T(8,128)(2,1)}, u32[]{:S(2)}) %copy-start.1) | copy-done | bytes 524312
  2.7 0.0 copy-start.2
  2.7 0.9 %copy-done.2 = bf16[1,128,1024]{2,1,0:T(8,128)(2,1)S(1)} copy-done((bf16[1,128,1024]{2,1,0:T(8,128)(2,1)S(1)}, bf16[1,128,1024]{2,1,0:T(8,128)(2,1)}, u32[]{:S(2)}) %copy-start.2) | copy-done | bytes 262168
  3.7 0.0 copy-start.3
  3.7 0.9 %copy-done.3 = bf16[1,128,1024]{2,1,0:T(8,128)(2,1)S(1)} copy-done((bf16[1,128,1024]{2,1,0:T(8,128)(2,1)S(1)}, bf16[1,128,1024]{2,1,0:T(8,128)(2,1)}, u32[]{:S(2)}) %copy-start.3) | copy-done | bytes 262168
  4.6 0.0 copy-start.4
  4.6 0.9 %copy-done.4 = bf16[1,128,1024]{2,1,0:T(8,128)(2,1)S(1)} copy-done((bf16[1,128,1024]{2,1,0:T(8,128)(2,1)S(1)}, bf16[1,128,1024]{2,1,0:T(8,128)(2,1)}, u32[]{:S(2)}) %copy-start.4) | copy-done | bytes 262168
  5.6 0.0 copy-start.5
  5.6 0.7 %copy-done.5 = s32[4,1,4]{2,1,0:T(1,128)S(1)} copy-done((s32[4,1,4]{2,1,0:T(1,128)S(1)}, s32[4,1,4]{2,1,0:T(1,128)}, u32[]{:S(2)}) %copy-start.5) | copy-done | bytes 88
  6.3 0.0 copy-start.6
  6.3 0.7 %copy-done.6 = s32[1,128]{1,0:T(1,128)S(1)} copy-done((s32[1,128]{1,0:T(1,128)S(1)}, s32[1,128]{1,0:T(1,128)}, u32[]{:S(2)}) %copy-start.6) | copy-done | bytes 536
  6.9 48.1 %shard_map.110 = (bf16[1,128,2048]{2,1,0:T(8,128)(2,1)S(1)}, bf16[1,128,1024]{2,1,0:T(8,128)(2,1)S(1)}, bf16[1,128,1024]{2,1,0:T(8,128)(2,1)S(1)}, bf16[1,128,20...) custom-call(s32[4,1,4]{2,1,0:T(1,128)S(1)} %copy-done.5, s32[1,128]{1,0:T(1,128)S(1)} %copy-done.6, ...), custom_call_target="tpu_custom_call" | custom-call | tf_op jit(solution)/shard_map/pallas_call | solution.py:379
  55.0 0.8 %copy.17 = bf16[1,128,2048]{2,1,0:T(8,128)(2,1)} copy(bf16[1,128,2048]{2,1,0:T(8,128)(2,1)S(1)} %get-tuple-element.10) | data formatting | bytes 1048576
  55.8 0.7 %copy.18 = bf16[1,128,1024]{2,1,0:T(8,128)(2,1)} copy(bf16[1,128,1024]{2,1,0:T(8,128)(2,1)S(1)} %get-tuple-element.11) | data formatting | bytes 524288
  56.5 0.7 %copy.19 = bf16[1,128,1024]{2,1,0:T(8,128)(2,1)} copy(bf16[1,128,1024]{2,1,0:T(8,128)(2,1)S(1)} %get-tuple-element.12) | data formatting | bytes 524288
  57.2 0.8 %copy.20 = bf16[1,128,2048]{2,1,0:T(8,128)(2,1)} copy(bf16[1,128,2048]{2,1,0:T(8,128)(2,1)S(1)} %get-tuple-element.13) | data formatting | bytes 1048576
  58.0 0.7 %copy.21 = bf16[1,128,1024]{2,1,0:T(8,128)(2,1)} copy(bf16[1,128,1024]{2,1,0:T(8,128)(2,1)S(1)} %get-tuple-element.14) | data formatting | bytes 524288
Async XLA Ops:
  0.6 1.0 %copy-start = (bf16[1,128,2048]{2,1,0:T(8,128)(2,1)S(1)}, bf16[1,128,2048]{2,1,0:T(8,128)(2,1)}, u32[]{:S(2)}) copy-start(bf16[1,128,2048]{2,1,0:T(8,128)(2,1)} %v_hbm.1) | copy-start | bytes 1572868
  1.7 1.0 %copy-start.1 = (bf16[1,128,2048]{2,1,0:T(8,128)(2,1)S(1)}, bf16[1,128,2048]{2,1,0:T(8,128)(2,1)}, u32[]{:S(2)}) copy-start(bf16[1,128,2048]{2,1,0:T(8,128)(2,1)} %g_hbm.1) | copy-start | bytes 1572868
  2.7 0.9 %copy-start.2 = (bf16[1,128,1024]{2,1,0:T(8,128)(2,1)S(1)}, bf16[1,128,1024]{2,1,0:T(8,128)(2,1)}, u32[]{:S(2)}) copy-start(bf16[1,128,1024]{2,1,0:T(8,128)(2,1)} %q_hbm.1) | copy-start | bytes 786436
  3.7 0.9 %copy-start.3 = (bf16[1,128,1024]{2,1,0:T(8,128)(2,1)S(1)}, bf16[1,128,1024]{2,1,0:T(8,128)(2,1)}, u32[]{:S(2)}) copy-start(bf16[1,128,1024]{2,1,0:T(8,128)(2,1)} %k_hbm.1) | copy-start | bytes 786436
  4.6 0.9 %copy-start.4 = (bf16[1,128,1024]{2,1,0:T(8,128)(2,1)S(1)}, bf16[1,128,1024]{2,1,0:T(8,128)(2,1)}, u32[]{:S(2)}) copy-start(bf16[1,128,1024]{2,1,0:T(8,128)(2,1)} %d_hbm.1) | copy-start | bytes 786436
  5.6 0.7 %copy-start.5 = (s32[4,1,4]{2,1,0:T(1,128)S(1)}, s32[4,1,4]{2,1,0:T(1,128)}, u32[]{:S(2)}) copy-start(s32[4,1,4]{2,1,0:T(1,128)} %order_hbm.1) | copy-start | bytes 196
  6.3 0.7 %copy-start.6 = (s32[1,128]{1,0:T(1,128)S(1)}, s32[1,128]{1,0:T(1,128)}, u32[]{:S(2)}) copy-start(s32[1,128]{1,0:T(1,128)} %doc_hbm.1) | copy-start | bytes 1540

commit v3 on v2

--- a/solution.py
+++ b/solution.py
@@ -46,9 +46,9 @@
 
 def kernel(
     n_dp, n_ctx, order_hbm, doc_hbm, q_hbm, k_hbm, v_hbm, d_hbm, g_hbm,
-    out_ref, dq_ref, dk_ref, dv_ref, dd_ref,
+    out_ref, ry,
     order_ref, doc_ref, q_ref, k_ref, v_ref, d_ref, g_ref, in_sem, decay,
-    sx, rx, sy, ry, f_own, f_in, b_own, b_in, doc_prev, doc_next,
+    sx, rx, sy, f_own, f_in, b_own, b_in, doc_prev, doc_next,
     x_send, x_recv, y_send, y_recv, f_send, f_recv, b_send, b_recv, doc_send, doc_recv,
 ):
     me = lax.axis_index("dp")
@@ -330,18 +330,6 @@
 
     lax.fori_loop(0, pairs, wait_back, 0)
 
-    def unpack(h, carry):
-        for dst, width, at in ((dq_ref, KW, 0), (dk_ref, KW, KW), (dd_ref, KW, 2 * KW), (dv_ref, VW, 3 * KW)):
-            parts = [ry[h, piece(j), at : at + width] for j in range(blocks)]
-            for j in range(blocks):
-                chosen = parts[0]
-                for place in range(1, blocks):
-                    chosen = lax.select(order[j] == place, parts[place], chosen)
-                dst[0, piece(j), lanes(h, width)] = chosen
-        return carry
-
-    lax.fori_loop(0, pairs, unpack, 0)
-
     def drain(h, carry):
         for r in range(1, n_dp):
             exchange(sx, rx, x_send, x_recv, h, r).wait_send()
@@ -366,6 +354,16 @@
     @pl.when(has_prev)
     def _():
         doc_down().wait_send()
+
+
+def unpack(pairs, order_ref, ry, rows_ref, out_ref, dq_ref, dk_ref, dv_ref, dd_ref):
+    out_ref[...] = rows_ref[...]
+    for h in range(pairs):
+        key, value = slice(h * KW, (h + 1) * KW), slice(h * VW, (h + 1) * VW)
+        dq_ref[0, :, key] = ry[h, :, 0:KW]
+        dk_ref[0, :, key] = ry[h, :, KW : 2 * KW]
+        dd_ref[0, :, key] = ry[h, :, 2 * KW : 3 * KW]
+        dv_ref[0, :, value] = ry[h, :, 3 * KW : W]
 
 
 def body(n_dp, n_ctx, query_rows, key_rows, value_rows, log_decay, out_grad, doc_ids, block_order):
@@ -376,11 +374,11 @@
     keys = jax.ShapeDtypeStruct((1, rows, hk), BF16)
     values = jax.ShapeDtypeStruct((1, rows, hv), BF16)
     dma = pltpu.SemaphoreType.DMA
-    out, dq, dk, dv, dd = pl.pallas_call(
+    rows_out, back = pl.pallas_call(
         functools.partial(kernel, n_dp, n_ctx),
-        out_shape=(values, keys, keys, values, keys),
+        out_shape=(values, jax.ShapeDtypeStruct((pairs, rows, W), BF16)),
         in_specs=[pl.BlockSpec(memory_space=pltpu.HBM)] * 7,
-        out_specs=(vmem,) * 5,
+        out_specs=(vmem,) * 2,
         scratch_shapes=[
             pltpu.SMEM(block_order.shape, jnp.int32),
             pltpu.VMEM((1, rows), jnp.int32),
@@ -391,7 +389,6 @@
             pltpu.VMEM((1, rows, hv), BF16),
             dma((7,)),
             pltpu.VMEM((pairs, KW, DV), F32),
-            pltpu.VMEM((pairs, rows, W), BF16),
             pltpu.VMEM((pairs, rows, W), BF16),
             pltpu.VMEM((pairs, rows, W), BF16),
             pltpu.VMEM((pairs, rows, W), BF16),
@@ -406,10 +403,24 @@
             dma((2,)), dma((2,)),
         ],
         compiler_params=pltpu.CompilerParams(
-            collective_id=0, has_side_effects=True, vmem_limit_bytes=40 * 1024 * 1024
+            collective_id=0, has_side_effects=True, vmem_limit_bytes=56 * 1024 * 1024
         ),
     )(block_order, doc_ids, query_rows, key_rows, value_rows, log_decay, out_grad)
-    return out, dq, dk, dv, dd
+    key_block = pl.BlockSpec((1, BLK, hk), lambda j, order: (0, j, 0))
+    value_block = pl.BlockSpec((1, BLK, hv), lambda j, order: (0, j, 0))
+    return pl.pallas_call(
+        functools.partial(unpack, pairs),
+        out_shape=(values, keys, keys, values, keys),
+        grid_spec=pltpu.PrefetchScalarGridSpec(
+            num_scalar_prefetch=1,
+            grid=(rows // BLK,),
+            in_specs=[
+                pl.BlockSpec((pairs, BLK, W), lambda j, order: (0, order[lax.axis_index("dp"), 0, j], 0)),
+                value_block,
+            ],
+            out_specs=(value_block, key_block, key_block, value_block, key_block),
+        ),
+    )(block_order, back, rows_out)
 
 
 def solution(mesh):

time: 59.1 us -> 54.4 us (0.920)
  local copies, waits for them, and re-layouts: 9.95 us -> 0 us
  Pallas kernels: 48.1 us -> 53.5 us
    unnamed x19 -> x0, local copies, waits for them, and re-layouts: 9.95 us -> none
    pallas_call x0 -> x1, Pallas kernels: none -> 4.39 us  [body(): pl.pallas_call(functools.partial(unpack, pairs), out_shape=(values, keys,...]
    pallas_call x1, Pallas kernels: 48.1 us -> 49.1 us  [body(): pl.pallas_call(functools.partial(kernel, n_dp, n_ctx), out_shape=(values,...]
where the time goes in v3:
time: 54.4 us; the launch traced here: 54.2 us
  Pallas kernels  53.5 us (98%)
  between operations  0.64 us (1%)
    pallas_call x1, Pallas kernels, body(): pl.pallas_call(functools.partial(kernel, n_dp, n_ctx), out_shape=(values,...  49.1 us
    pallas_call x1, Pallas kernels, body(): pl.pallas_call(functools.partial(unpack, pairs), out_shape=(values, keys,...  4.39 us

profile of v3, /device:TPU:0, one launch (start us, length us, event | category | flops | bytes accessed | tf_op | source)
XLA Modules:
  0.0 54.2 jit_solution(326700618786063243)
XLA Ops:
  0.6 49.1 %shard_map.110 = (bf16[1,128,2048]{2,1,0:T(8,128)(2,1)}, bf16[8,128,640]{2,1,0:T(8,128)(2,1)}) custom-call(s32[4,1,4]{2,1,0:T(1,128)} %order_ref.1, s32[1,128]{1,0:T(1,128)} %doc_hbm.1, bf16[1,128,1024]{2,1,0:T(8,128)(2,1)} %q_hbm.1, bf16[1,128,1024]{2,1,0:T(8,128)(2,1)} %k_hbm.1, bf16[1,128,2048]{2,1,0:T(8,128)(2,1)} %v_hbm.1, bf16[1,128,1024]{2,1,0:T(8,128)(2,1)} %d_hbm.1, ...), custom_call_target="tpu_custom_call" | custom-call | tf_op jit(solution)/shard_map/pallas_call | solution.py:377
  49.8 4.4 %shard_map.111 = (bf16[1,128,2048]{2,1,0:T(8,128)(2,1)}, bf16[1,128,1024]{2,1,0:T(8,128)(2,1)}, bf16[1,128,1024]{2,1,0:T(8,128)(2,1)}, bf16[1,128,2048]{2,1,0:T(8,128)(2,1)}, bf16[1,128,1024]{2,1,0:T(8,128)(2,1)}) custom-call(s32[4,1,4]{2,1,0:T(1,128)} %order_ref.1, bf16[8,128,640]{2,1,0:T(8,128)(2,1)} %get-tuple-element.7.ry, ...), custom_call_target="tpu_custom_call" | custom-call | tf_op jit(solution)/shard_map/pallas_call | solution.py:411

commit v4 on v3

--- a/solution.py
+++ b/solution.py
@@ -47,7 +47,7 @@
 def kernel(
     n_dp, n_ctx, order_hbm, doc_hbm, q_hbm, k_hbm, v_hbm, d_hbm, g_hbm,
     out_ref, ry,
-    order_ref, doc_ref, q_ref, k_ref, v_ref, d_ref, g_ref, in_sem, decay,
+    order_ref, doc_ref, q_ref, k_ref, v_ref, d_ref, g_ref, in_sem, decay, near, dv_near, dq_near, dk_near,
     sx, rx, sy, f_own, f_in, b_own, b_in, doc_prev, doc_next,
     x_send, x_recv, y_send, y_recv, f_send, f_recv, b_send, b_recv, doc_send, doc_recv,
 ):
@@ -240,11 +240,10 @@
         b_own[h] = factor * fold(dot(split(q_f * growth * in_first), g, TN))
         decay[h] = jnp.exp(dot(d, jnp.ones((rows, DV), BF16), TN))
 
-    def finish(h):
+    def inside(h):
         q_f, k_f, v, g, d, growth, shrink, to_end = load(h)
         q_t = q_f * growth
         k_t = k_f * shrink
-        k_e = k_f * to_end * tail_w
         zero = jnp.zeros_like(q_t)
         q_2 = split(jnp.concatenate([jnp.where(in_a, q_t, zero), jnp.where(in_a, zero, q_t)], axis=0))
         k_s = split(k_t)
@@ -255,19 +254,26 @@
         g_a, g_b = g[:, 0:DV], g[:, DV:VW]
         score_a = both(lambda x: x[0:rows], score_2)
         score_b = both(lambda x: x[rows : 2 * rows], score_2)
+        near[h, :, 0:DV] = dot(score_a, v_a, NN)
+        near[h, :, DV:VW] = dot(score_b, v_b, NN)
+        dv_near[h, :, 0:DV] = dot(score_a, g_a, TN)
+        dv_near[h, :, DV:VW] = dot(score_b, g_b, TN)
+        gs_a = jnp.where(same, dot(g_a, v_a, NT), 0.0)
+        gs_b = jnp.where(same, dot(g_b, v_b, NT), 0.0)
+        dq_near[h] = dot(split(jnp.concatenate([gs_a, gs_b], axis=1)), k_2, NN)
+        dk_near[h] = factor * shrink * dot(split(jnp.concatenate([gs_a, gs_b], axis=0)), q_2, TN)
+
+    def finish(h):
+        q_f, k_f, v, g, d, growth, shrink, to_end = load(h)
+        q_t = q_f * growth
+        k_e = k_f * to_end * tail_w
         state = both(spread, split(f_in[h]))
         carry = both(spread, split(b_in[h]))
-        near = jnp.concatenate([dot(score_a, v_a, NN), dot(score_b, v_b, NN)], axis=1)
         far = dot(split(q_t * head_w), state, NN)
-        out_ref[0, :, lanes(h, VW)] = (factor * (near + far)).astype(BF16)
-        gs_a = jnp.where(same, dot(g_a, v_a, NT), 0.0)
-        gs_b = jnp.where(same, dot(g_b, v_b, NT), 0.0)
-        dq_near = dot(split(jnp.concatenate([gs_a, gs_b], axis=1)), k_2, NN)
-        dq = factor * growth * (dq_near + dot(g, state, NT) * head_w)
-        dk_near = dot(split(jnp.concatenate([gs_a, gs_b], axis=0)), q_2, TN)
-        dk = factor * shrink * dk_near + to_end * dot(v, carry, NT) * tail_w
-        dv_near = jnp.concatenate([dot(score_a, g_a, TN), dot(score_b, g_b, TN)], axis=1)
-        dv = factor * dv_near + dot(split(k_e), carry, NN)
+        out_ref[0, :, lanes(h, VW)] = (factor * (near[h] + far)).astype(BF16)
+        dq = factor * growth * (dq_near[h] + dot(g, state, NT) * head_w)
+        dk = dk_near[h] + to_end * dot(v, carry, NT) * tail_w
+        dv = factor * dv_near[h] + dot(split(k_e), carry, NN)
         log_grad = q_f * dq - k_f * dk
         sums = dot(jnp.ones((8, DV), BF16), split(f_own[h] * b_in[h]), NT)
         dd = dot(later, split(log_grad), NN) + sums[0:1] * tail_w
@@ -311,13 +317,17 @@
             def _():
                 chain_down(down).start()
 
+        @pl.when((t >= 1) & (t <= pairs))
+        def _():
+            inside(t - 1)
+
+        @pl.when((ready >= 0) & (ready < pairs))
+        def _():
+            finish(ready)
+
         @pl.when(t < pairs)
         def _():
             local(t)
-
-        @pl.when((ready >= 0) & (ready < pairs))
-        def _():
-            finish(ready)
 
         return carry
 
@@ -389,6 +399,10 @@
             pltpu.VMEM((1, rows, hv), BF16),
             dma((7,)),
             pltpu.VMEM((pairs, KW, DV), F32),
+            pltpu.VMEM((pairs, rows, VW), F32),
+            pltpu.VMEM((pairs, rows, VW), F32),
+            pltpu.VMEM((pairs, rows, KW), F32),
+            pltpu.VMEM((pairs, rows, KW), F32),
             pltpu.VMEM((pairs, rows, W), BF16),
             pltpu.VMEM((pairs, rows, W), BF16),
             pltpu.VMEM((pairs, rows, W), BF16),

time: 54.4 us -> 53.8 us (0.989)
  Pallas kernels: 53.5 us -> 52.9 us
    pallas_call x1, Pallas kernels: 49.1 us -> 48.6 us  [body(): pl.pallas_call(functools.partial(kernel, n_dp, n_ctx), out_shape=(values,...]
where the time goes in v4:
time: 53.8 us; the launch traced here: 53.6 us
  Pallas kernels  52.9 us (98%)
  between operations  0.64 us (1%)
    pallas_call x1, Pallas kernels, body(): pl.pallas_call(functools.partial(kernel, n_dp, n_ctx), out_shape=(values,...  48.6 us
    pallas_call x1, Pallas kernels, body(): pl.pallas_call(functools.partial(unpack, pairs), out_shape=(values, keys,...  4.39 us

profile of v4, /device:TPU:0, one launch (start us, length us, event | category | flops | bytes accessed | tf_op | source)
XLA Modules:
  0.0 53.6 jit_solution(7840411578507525555)
XLA Ops:
  0.6 48.6 %shard_map.110 = (bf16[1,128,2048]{2,1,0:T(8,128)(2,1)}, bf16[8,128,640]{2,1,0:T(8,128)(2,1)}) custom-call(s32[4,1,4]{2,1,0:T(1,128)} %order_ref.1, s32[1,128]{1,0:T(1,128)} %doc_hbm.1, bf16[1,128,1024]{2,1,0:T(8,128)(2,1)} %q_hbm.1, bf16[1,128,1024]{2,1,0:T(8,128)(2,1)} %k_hbm.1, bf16[1,128,2048]{2,1,0:T(8,128)(2,1)} %v_hbm.1, bf16[1,128,1024]{2,1,0:T(8,128)(2,1)} %d_hbm.1, ...), custom_call_target="tpu_custom_call" | custom-call | tf_op jit(solution)/shard_map/pallas_call | solution.py:387
  49.2 4.4 %shard_map.111 = (bf16[1,128,2048]{2,1,0:T(8,128)(2,1)}, bf16[1,128,1024]{2,1,0:T(8,128)(2,1)}, bf16[1,128,1024]{2,1,0:T(8,128)(2,1)}, bf16[1,128,2048]{2,1,0:T(8,128)(2,1)}, bf16[1,128,1024]{2,1,0:T(8,128)(2,1)}) custom-call(s32[4,1,4]{2,1,0:T(1,128)} %order_ref.1, bf16[8,128,640]{2,1,0:T(8,128)(2,1)} %get-tuple-element.7.ry, ...), custom_call_target="tpu_custom_call" | custom-call | tf_op jit(solution)/shard_map/pallas_call | solution.py:425

commit v5 on v4

--- a/solution.py
+++ b/solution.py
@@ -366,14 +366,34 @@
         doc_down().wait_send()
 
 
-def unpack(pairs, order_ref, ry, rows_ref, out_ref, dq_ref, dk_ref, dv_ref, dd_ref):
-    out_ref[...] = rows_ref[...]
-    for h in range(pairs):
-        key, value = slice(h * KW, (h + 1) * KW), slice(h * VW, (h + 1) * VW)
-        dq_ref[0, :, key] = ry[h, :, 0:KW]
-        dk_ref[0, :, key] = ry[h, :, KW : 2 * KW]
-        dd_ref[0, :, key] = ry[h, :, 2 * KW : 3 * KW]
-        dv_ref[0, :, value] = ry[h, :, 3 * KW : W]
+def unpack(pairs, order_ref, ry, rows_ref, out_ref, dq_ref, dk_ref, dv_ref, dd_ref,
+           buf, dq_v, dk_v, dv_v, dd_v, in_sem, out_sem, rows_sem):
+    me = lax.axis_index("dp")
+    blocks = rows_ref.shape[1] // BLK
+    across = pltpu.make_async_copy(rows_ref, out_ref, rows_sem)
+    fetches = []
+    for j in range(blocks):
+        here = pl.ds(pl.multiple_of(order_ref[me, 0, j] * BLK, BLK), BLK)
+        fetches.append(pltpu.make_async_copy(ry.at[:, here, :], buf.at[j], in_sem.at[j]))
+        fetches[j].start()
+    across.start()
+    stores = []
+    for j in range(blocks):
+        fetches[j].wait()
+        there = slice(j * BLK, (j + 1) * BLK)
+        for h in range(pairs):
+            key, value = slice(h * KW, (h + 1) * KW), slice(h * VW, (h + 1) * VW)
+            dq_v[0, there, key] = buf[j, h, :, 0:KW]
+            dk_v[0, there, key] = buf[j, h, :, KW : 2 * KW]
+            dd_v[0, there, key] = buf[j, h, :, 2 * KW : 3 * KW]
+            dv_v[0, there, value] = buf[j, h, :, 3 * KW : W]
+        for i, (src, dst) in enumerate(((dq_v, dq_ref), (dk_v, dk_ref), (dv_v, dv_ref), (dd_v, dd_ref))):
+            store = pltpu.make_async_copy(src.at[:, there, :], dst.at[:, there, :], out_sem.at[j, i])
+            store.start()
+            stores.append(store)
+    for store in stores:
+        store.wait()
+    across.wait()
 
 
 def body(n_dp, n_ctx, query_rows, key_rows, value_rows, log_decay, out_grad, doc_ids, block_order):
@@ -420,20 +440,19 @@
             collective_id=0, has_side_effects=True, vmem_limit_bytes=56 * 1024 * 1024
         ),
     )(block_order, doc_ids, query_rows, key_rows, value_rows, log_decay, out_grad)
-    key_block = pl.BlockSpec((1, BLK, hk), lambda j, order: (0, j, 0))
-    value_block = pl.BlockSpec((1, BLK, hv), lambda j, order: (0, j, 0))
+    hbm = pl.BlockSpec(memory_space=pltpu.HBM)
+    key_rows_v, value_rows_v = pltpu.VMEM((1, rows, hk), BF16), pltpu.VMEM((1, rows, hv), BF16)
     return pl.pallas_call(
         functools.partial(unpack, pairs),
         out_shape=(values, keys, keys, values, keys),
-        grid_spec=pltpu.PrefetchScalarGridSpec(
-            num_scalar_prefetch=1,
-            grid=(rows // BLK,),
-            in_specs=[
-                pl.BlockSpec((pairs, BLK, W), lambda j, order: (0, order[lax.axis_index("dp"), 0, j], 0)),
-                value_block,
-            ],
-            out_specs=(value_block, key_block, key_block, value_block, key_block),
-        ),
+        in_specs=[pl.BlockSpec(memory_space=pltpu.SMEM), hbm, hbm],
+        out_specs=(hbm,) * 5,
+        scratch_shapes=[
+            pltpu.VMEM((rows // BLK, pairs, BLK, W), BF16),
+            key_rows_v, key_rows_v, value_rows_v, key_rows_v,
+            dma((rows // BLK,)), dma((rows // BLK, 4)), dma,
+        ],
+        compiler_params=pltpu.CompilerParams(vmem_limit_bytes=56 * 1024 * 1024),
     )(block_order, back, rows_out)
 
 

time: 53.8 us -> 67.3 us (1.25)
  Pallas kernels: 52.9 us -> 66.4 us
    pallas_call x1, Pallas kernels: 4.39 us -> 17.9 us  [body(): pl.pallas_call(functools.partial(unpack, pairs), out_shape=(values, keys,...]
where the time goes in v5:
time: 67.3 us; the launch traced here: 67.1 us
  Pallas kernels  66.4 us (99%)
    pallas_call x1, Pallas kernels, body(): pl.pallas_call(functools.partial(kernel, n_dp, n_ctx), out_shape=(values,...  48.6 us
    pallas_call x1, Pallas kernels, body(): pl.pallas_call(functools.partial(unpack, pairs), out_shape=(values, keys,...  17.9 us

profile of v5, /device:TPU:0, one launch (start us, length us, event | category | flops | bytes accessed | tf_op | source)
XLA Modules:
  0.0 67.1 jit_solution(3806274129668840860)
XLA Ops:
  0.6 48.6 %shard_map.110 = (bf16[1,128,2048]{2,1,0:T(8,128)(2,1)}, bf16[8,128,640]{2,1,0:T(8,128)(2,1)}) custom-call(s32[4,1,4]{2,1,0:T(1,128)} %order_ref.1, s32[1,128]{1,0:T(1,128)} %doc_hbm.1, bf16[1,128,1024]{2,1,0:T(8,128)(2,1)} %q_hbm.1, bf16[1,128,1024]{2,1,0:T(8,128)(2,1)} %k_hbm.1, bf16[1,128,2048]{2,1,0:T(8,128)(2,1)} %v_hbm.1, bf16[1,128,1024]{2,1,0:T(8,128)(2,1)} %d_hbm.1, ...), custom_call_target="tpu_custom_call" | custom-call | tf_op jit(solution)/shard_map/pallas_call | solution.py:407
  49.2 17.9 %shard_map.111 = (bf16[1,128,2048]{2,1,0:T(8,128)(2,1)}, bf16[1,128,1024]{2,1,0:T(8,128)(2,1)}, bf16[1,128,1024]{2,1,0:T(8,128)(2,1)}, bf16[1,128,2048]{2,1,0:T(8,128)(2,1)}, bf16[1,128,1024]{2,1,0:T(8,128)(2,1)}) custom-call(s32[4,1,4]{2,1,0:T(1,128)} %order_ref.1, bf16[8,128,640]{2,1,0:T(8,128)(2,1)} %get-tuple-element.7.ry, ...), custom_call_target="tpu_custom_call" | custom-call | tf_op jit(solution)/shard_map/pallas_call | solution.py:445

commit v6 on v5

--- a/solution.py
+++ b/solution.py
@@ -367,16 +367,19 @@
 
 
 def unpack(pairs, order_ref, ry, rows_ref, out_ref, dq_ref, dk_ref, dv_ref, dd_ref,
-           buf, dq_v, dk_v, dv_v, dd_v, in_sem, out_sem, rows_sem):
+           buf, rows_v, dq_v, dk_v, dv_v, dd_v, in_sem, out_sem, rows_sem):
     me = lax.axis_index("dp")
     blocks = rows_ref.shape[1] // BLK
-    across = pltpu.make_async_copy(rows_ref, out_ref, rows_sem)
+    rows_in = pltpu.make_async_copy(rows_ref, rows_v, rows_sem.at[0])
+    rows_in.start()
+    rows_out = pltpu.make_async_copy(rows_v, out_ref, rows_sem.at[1])
     fetches = []
     for j in range(blocks):
         here = pl.ds(pl.multiple_of(order_ref[me, 0, j] * BLK, BLK), BLK)
         fetches.append(pltpu.make_async_copy(ry.at[:, here, :], buf.at[j], in_sem.at[j]))
         fetches[j].start()
-    across.start()
+    rows_in.wait()
+    rows_out.start()
     stores = []
     for j in range(blocks):
         fetches[j].wait()
@@ -393,7 +396,7 @@
             stores.append(store)
     for store in stores:
         store.wait()
-    across.wait()
+    rows_out.wait()
 
 
 def body(n_dp, n_ctx, query_rows, key_rows, value_rows, log_decay, out_grad, doc_ids, block_order):
@@ -449,8 +452,8 @@
         out_specs=(hbm,) * 5,
         scratch_shapes=[
             pltpu.VMEM((rows // BLK, pairs, BLK, W), BF16),
-            key_rows_v, key_rows_v, value_rows_v, key_rows_v,
-            dma((rows // BLK,)), dma((rows // BLK, 4)), dma,
+            value_rows_v, key_rows_v, key_rows_v, value_rows_v, key_rows_v,
+            dma((rows // BLK,)), dma((rows // BLK, 4)), dma((2,)),
         ],
         compiler_params=pltpu.CompilerParams(vmem_limit_bytes=56 * 1024 * 1024),
     )(block_order, back, rows_out)

time: 67.3 us -> 52.5 us (0.78)
  Pallas kernels: 66.4 us -> 51.7 us
    pallas_call x1, Pallas kernels: 17.9 us -> 3.14 us  [body(): pl.pallas_call(functools.partial(unpack, pairs), out_shape=(values, keys,...]
where the time goes in v6:
time: 52.5 us; the launch traced here: 52.3 us
  Pallas kernels  51.7 us (98%)
  between operations  0.64 us (1%)
    pallas_call x1, Pallas kernels, body(): pl.pallas_call(functools.partial(kernel, n_dp, n_ctx), out_shape=(values,...  48.6 us
    pallas_call x1, Pallas kernels, body(): pl.pallas_call(functools.partial(unpack, pairs), out_shape=(values, keys,...  3.14 us

profile of v6, /device:TPU:0, one launch (start us, length us, event | category | flops | bytes accessed | tf_op | source)
XLA Modules:
  0.0 52.3 jit_solution(1253670300203260186)
XLA Ops:
  0.6 48.6 %shard_map.110 = (bf16[1,128,2048]{2,1,0:T(8,128)(2,1)}, bf16[8,128,640]{2,1,0:T(8,128)(2,1)}) custom-call(s32[4,1,4]{2,1,0:T(1,128)} %order_ref.1, s32[1,128]{1,0:T(1,128)} %doc_hbm.1, bf16[1,128,1024]{2,1,0:T(8,128)(2,1)} %q_hbm.1, bf16[1,128,1024]{2,1,0:T(8,128)(2,1)} %k_hbm.1, bf16[1,128,2048]{2,1,0:T(8,128)(2,1)} %v_hbm.1, bf16[1,128,1024]{2,1,0:T(8,128)(2,1)} %d_hbm.1, ...), custom_call_target="tpu_custom_call" | custom-call | tf_op jit(solution)/shard_map/pallas_call | solution.py:410
  49.2 3.1 %shard_map.111 = (bf16[1,128,2048]{2,1,0:T(8,128)(2,1)}, bf16[1,128,1024]{2,1,0:T(8,128)(2,1)}, bf16[1,128,1024]{2,1,0:T(8,128)(2,1)}, bf16[1,128,2048]{2,1,0:T(8,128)(2,1)}, bf16[1,128,1024]{2,1,0:T(8,128)(2,1)}) custom-call(s32[4,1,4]{2,1,0:T(1,128)} %order_ref.1, bf16[8,128,640]{2,1,0:T(8,128)(2,1)} %get-tuple-element.7.ry, ...), custom_call_target="tpu_custom_call" | custom-call | tf_op jit(solution)/shard_map/pallas_call | solution.py:448
